TPU v7x, 32 devices: a whole 2x2x4 slice. The times are simulated.
32 devices in a mesh: row: 8 (over z, core), col: 4 (over y, x).
Axes of the slice: x: 2, y: 2, z: 4, core: 2. Of those that a mesh axis runs over, the one named last changes fastest.
Arguments:
- atom_feats: bfloat16 [5120, 128], P(('row', 'col')), may hold values from -6 to 6
- atom_bias: float32 [4, 5120, 128], P(None, ('row', 'col')), may hold values from -5 to 360
- atom_counts: int32 [1280], replicated, may hold values from 1 to 24, 5120 in all
- valid_tokens: int32 [1], replicated, may hold values from 640 to 1280
- pair_in: bfloat16 [256, 1280, 128], P('row', 'col'), may hold values from -6 to 6
- atom_gain: float32 [128], replicated, may hold values from 0.5 to 1.5
- atom_proj: bfloat16 [128, 512], replicated, may hold values from -0.5 to 0.5
- atom_out: bfloat16 [128, 128], replicated, may hold values from -4 to 4
- atom_pool: bfloat16 [128, 384], replicated, may hold values from -0.5 to 0.5
- single_to_pair: bfloat16 [384, 256], replicated, may hold values from -0.3125 to 0.3125
- pair_gains: float32 [3, 128], replicated, may hold values from 0.5 to 1.5
- trans_in: bfloat16 [128, 1024], replicated, may hold values from -0.5 to 0.5
- trans_out: bfloat16 [512, 128], replicated, may hold values from -0.25 to 0.25
- tri_in: bfloat16 [128, 512], replicated, may hold values from -0.5 to 0.5
- tri_out: bfloat16 [128, 128], replicated, may hold values from -0.5 to 0.5
Outputs:
- single: bfloat16 [1280, 384], P('col')
- update: bfloat16 [256, 256, 128], P('row', 'col')
Inputs may be any that keep to these rules, and one draw needn't show every extreme that they name: `atom_counts`: the counts sum to 5120; some token has exactly 24 atoms.
All inputs are finite; a program needn't handle non-finite values.
Results may differ from a plain program's by a relative error of at most 0.0091.
Values may be sent and summed in bfloat16 or wider, within the bound.
No kernel may reach another device: no remote copies, remote signals or barrier semaphores. Data moves between devices by JAX's collectives and lax.ppermute only.
A program may use at most 128 MiB of HBM per device.

v0:
```python
import jax
import jax.numpy as jnp
from jax import lax
from jax.sharding import PartitionSpec as P

QBLOCK = 32
KEYS = 128
RIM = 48
EPS = 1e-05


def padded(shard, sides, width):
    for axis, dim in sides:
        size, length = (lax.axis_size(axis), shard.shape[dim])
        up = [(i, (i + 1) % size) for i in range(size - 1)]
        down = [(j, i) for i, j in up]
        last = lax.slice_in_dim(shard, length - width, length, axis=dim)
        initial = lax.slice_in_dim(shard, 0, width, axis=dim)
        before = lax.ppermute(last, axis, up)
        after = lax.ppermute(initial, axis, down)
        shard = jnp.concatenate([before, shard, after], axis=dim)
    return shard


def normalize(values, gain_row):
    values = values.astype(jnp.float32)
    average = jnp.mean(values, axis=-1, keepdims=True)
    centered = values - average
    variance = jnp.mean(centered * centered, axis=-1, keepdims=True)
    return centered * lax.rsqrt(variance + EPS) * gain_row


def attend(queries, key_vals, gating, atom_bias, first_atom, total_atoms):
    atom_rows, atom_width = queries.shape
    blocks = atom_rows // QBLOCK
    head_count = atom_bias.shape[0]
    head_size = atom_width // head_count
    windowed = jnp.stack(
        [key_vals[QBLOCK * block_id : QBLOCK * block_id + KEYS] for block_id in range(blocks)]
    )
    position = (
        first_atom
        - RIM
        + (jnp.arange(blocks, dtype=jnp.int32) * QBLOCK)[:, None]
        + jnp.arange(KEYS, dtype=jnp.int32)[None, :]
    )
    in_range = (position >= 0) & (position < total_atoms)
    query_heads = queries.reshape(blocks, QBLOCK, head_count, head_size)
    key_heads = windowed[:, :, :atom_width].reshape(blocks, KEYS, head_count, head_size)
    value_heads = windowed[:, :, atom_width:].reshape(blocks, KEYS, head_count, head_size)
    scores = jnp.einsum(
        "bqhd,bkhd->bhqk", query_heads, key_heads, preferred_element_type=jnp.float32
    ) * head_size ** (-0.5)
    bias_rows = atom_bias.reshape(head_count, blocks, QBLOCK, KEYS).transpose(1, 0, 2, 3)
    scores = jnp.where(in_range[:, None, None, :], scores + bias_rows, -1e30)
    row_max = jnp.max(scores, axis=-1, keepdims=True)
    exponent = jnp.exp(scores - row_max)
    weights = (exponent / jnp.sum(exponent, axis=-1, keepdims=True)).astype(jnp.bfloat16)
    blended = jnp.einsum(
        "bhqk,bkhd->bqhd", weights, value_heads, preferred_element_type=jnp.float32
    )
    return (blended.reshape(atom_rows, atom_width) * gating).astype(jnp.bfloat16)


def body(
    atom_feats,
    atom_bias,
    atom_counts,
    valid_tokens,
    pair_in,
    atom_gain,
    atom_proj,
    atom_out,
    atom_pool,
    single_to_pair,
    pair_gains,
    trans_in,
    trans_out,
    tri_in,
    tri_out,
):
    atom_rows, atom_width = atom_feats.shape
    position = lax.axis_index(("row", "col"))
    total_atoms = atom_rows * lax.axis_size(("row", "col"))
    first_atom = position * atom_rows
    normed = normalize(atom_feats, atom_gain).astype(jnp.bfloat16)
    projected = jnp.dot(normed, atom_proj, preferred_element_type=jnp.float32)
    queries = projected[:, :atom_width].astype(jnp.bfloat16)
    gating = jax.nn.sigmoid(projected[:, 3 * atom_width :])
    key_vals = projected[:, atom_width : 3 * atom_width].astype(jnp.bfloat16)
    key_vals = padded(key_vals, ((("row", "col"), 0),), RIM)
    gated = attend(queries, key_vals, gating, atom_bias, first_atom, total_atoms)
    updated = (
        atom_feats.astype(jnp.float32)
        + jnp.dot(gated, atom_out, preferred_element_type=jnp.float32)
    ).astype(jnp.bfloat16)
    hidden = jax.nn.relu(jnp.dot(updated, atom_pool, preferred_element_type=jnp.float32))
    tokens = atom_counts.shape[0]
    token_ends = jnp.cumsum(atom_counts)
    starts = token_ends - atom_counts
    atom_index = first_atom + jnp.arange(atom_rows, dtype=jnp.int32)
    owners = jnp.sum((starts[None, :] <= atom_index[:, None]).astype(jnp.int32), axis=1) - 1
    first_token = owners[0]
    offsets = owners - first_token
    onehot = (offsets[None, :] == jnp.arange(atom_rows, dtype=jnp.int32)[:, None]).astype(
        jnp.float32
    )
    window = jnp.dot(onehot, hidden, precision=lax.Precision.HIGHEST)
    table_sums = jnp.zeros((tokens + atom_rows, hidden.shape[1]), jnp.float32)
    table_sums = lax.dynamic_update_slice_in_dim(table_sums, window, first_token, 0)[:tokens]
    count_float = atom_counts.astype(jnp.float32)
    totals = lax.psum(table_sums, ("row", "col"))
    single_all = (totals / count_float[:, None]).astype(jnp.bfloat16)
    row_dev, tok_col, channels = pair_in.shape
    col_place = lax.axis_index("col")
    row_place = lax.axis_index("row")
    single = lax.dynamic_slice_in_dim(single_all, col_place * tok_col, tok_col)
    row_single = lax.dynamic_slice_in_dim(single_all, row_place * row_dev, row_dev)
    row_terms = jnp.dot(
        row_single, single_to_pair[:, :channels], preferred_element_type=jnp.float32
    )
    col_terms = jnp.dot(single, single_to_pair[:, channels:], preferred_element_type=jnp.float32)
    col_mask = (
        col_place * tok_col + jnp.arange(tok_col, dtype=jnp.int32) < valid_tokens[0]
    ).astype(jnp.float32)[:, None]

    def pair_row(operands):
        row_in, row_add = operands
        paired = (row_in.astype(jnp.float32) + row_add[None, :] + col_terms).astype(jnp.bfloat16)
        normed_row = normalize(paired, pair_gains[0]).astype(jnp.bfloat16)
        gate_up = jnp.dot(normed_row, trans_in, preferred_element_type=jnp.float32)
        inner = (jax.nn.silu(gate_up[:, : 4 * channels]) * gate_up[:, 4 * channels :]).astype(
            jnp.bfloat16
        )
        paired = (
            paired.astype(jnp.float32)
            + jnp.dot(inner, trans_out, preferred_element_type=jnp.float32)
        ).astype(jnp.bfloat16)
        normed_row = normalize(paired, pair_gains[1]).astype(jnp.bfloat16)
        tri_proj = jnp.dot(normed_row, tri_in, preferred_element_type=jnp.float32)
        left_row = (
            jax.nn.sigmoid(tri_proj[:, :channels]) * tri_proj[:, channels : 2 * channels] * col_mask
        ).astype(jnp.bfloat16)
        right_row = (
            jax.nn.sigmoid(tri_proj[:, 2 * channels : 3 * channels])
            * tri_proj[:, 3 * channels :]
            * col_mask
        ).astype(jnp.bfloat16)
        return (left_row, right_row)

    left_ops, right_ops = lax.map(pair_row, (pair_in, row_terms))
    partial_value = jnp.einsum(
        "ikc,jkc->ijc",
        left_ops,
        lax.all_gather(right_ops, "row", axis=0, tiled=True),
        preferred_element_type=jnp.float32,
    )
    summed = lax.psum_scatter(partial_value, "col", scatter_dimension=1, tiled=True)
    normed_out = normalize(summed, pair_gains[2]).astype(jnp.bfloat16)
    update = jnp.dot(normed_out.reshape(-1, channels), tri_out, preferred_element_type=jnp.float32)
    update = update.reshape(summed.shape).astype(jnp.bfloat16)
    return (single, update)


def solution(mesh):
    in_specs = (
        P(("row", "col"), None),
        P(None, ("row", "col"), None),
        P(),
        P(),
        P("row", "col", None),
        P(),
        P(),
        P(),
        P(),
        P(),
        P(),
        P(),
        P(),
        P(),
        P(),
    )
    out_specs = (P("col", None), P("row", "col", None))
    return jax.shard_map(body, mesh=mesh, in_specs=in_specs, out_specs=out_specs, check_vma=False)
```

profile of v0, /device:TPU:0, one launch (start us, length us, event | category | flops | bytes accessed | tf_op | source)
XLA Modules:
  0.0 658.5 jit_solution(9790463930272878575)
XLA Ops:
  10.2 4.8 collective-permute-start
  15.1 1.3 collective-permute-start.1
  23.1 1.2 convolution_bitcast_fusion.1
  25.4 1.8 dynamic_update_slice.10
  27.2 1.4 slice.138
  28.7 135.9 %all-reduce.2.cloned.1.call-done = f32[1280,384]{1,0:T(8,128)} async-done(((f32[1280,384]{1,0:T(8,128)}), f32[1280,384]{1,0:T(8,128)}) %all-reduce.2.cloned.1.call-update) | async-done | bytes 1966096 | tf_op jit(solution)/shard_map/psum | solution.py:112
  164.6 1.8 divide_convert_fusion
  166.4 1.2 fusion.46
  167.6 1.6 fusion.48
  169.3 184.3 %while.13 = (s32[]{:T(128)}, bf16[32,320,128]{2,1,0:T(8,128)(2,1)}, bf16[32,320,128]{2,1,0:T(8,128)(2,1)S(1)}, bf16[32,320,128]{2,1,0:T(8,128)(2,1)}, f32[32,128...) while((s32[]{:T(128)}, bf16[32,320,128]{2,1,0:T(8,128)(2,1)}, ...), condition=%wide.region_13.14_spmd.clone, body=%wide.region_8.13_spmd.clone.sunk | while | flops 170354240 | bytes 5716877 | solution.py:151
  170.1 1.0 convert_reduce_fusion.4
  171.7 1.3 fusion.127
  177.5 1.3 fusion.127
  181.6 1.0 convert_reduce_fusion.4
  183.3 1.3 fusion.127
  187.3 1.0 convert_reduce_fusion.4
  189.0 1.3 fusion.127
  194.8 1.3 fusion.127
  198.9 1.0 convert_reduce_fusion.4
  200.5 1.3 fusion.127
  204.6 1.0 convert_reduce_fusion.4
  206.3 1.3 fusion.127
  210.4 1.0 convert_reduce_fusion.4
  212.0 1.3 fusion.127
  216.1 1.0 convert_reduce_fusion.4
  217.8 1.3 fusion.127
  221.9 1.0 convert_reduce_fusion.4
  223.6 1.3 fusion.127
  227.6 1.0 convert_reduce_fusion.4
  229.3 1.3 fusion.127
  233.4 1.0 convert_reduce_fusion.4
  235.1 1.3 fusion.127
  239.1 1.0 convert_reduce_fusion.4
  240.8 1.3 fusion.127
  244.9 1.0 convert_reduce_fusion.4
  246.6 1.3 fusion.127
  252.3 1.3 fusion.127
  256.4 1.0 convert_reduce_fusion.4
  258.1 1.3 fusion.127
  263.9 1.3 fusion.127
  269.6 1.3 fusion.127
  275.4 1.3 fusion.127
  281.2 1.3 fusion.127
  286.9 1.3 fusion.127
  292.7 1.3 fusion.127
  298.4 1.3 fusion.127
  304.2 1.3 fusion.127
  310.0 1.3 fusion.127
  315.7 1.3 fusion.127
  321.5 1.3 fusion.127
  327.2 1.3 fusion.127
  333.0 1.3 fusion.127
  338.8 1.3 fusion.127
  344.5 1.3 fusion.127
  350.3 1.3 fusion.127
  353.6 3.4 copy.46
  357.1 3.8 copy.47
  361.0 215.0 %all-gather.2.cloned.1.call-done = bf16[256,320,128]{1,0,2:T(8,128)(2,1)} async-done(((bf16[32,320,128]{1,0,2:T(8,128)(2,1)}), bf16[256,320,128]{1,0,2:T(8,128)(2,1)}) %all-gather.2.cloned.1.call-update) | async-done | bytes 20971536 | tf_op jit(solution)/shard_map/all_gather | solution.py:155
  575.9 13.8 %convolution_bitcast_fusion = f32[32,256,128]{1,0,2:T(8,128)} fusion(bf16[256,320,128]{1,0,2:T(8,128)(2,1)} %all-gather.2.cloned.1.call-done, bf16[32,320,128]{1,0,2:T(8,128)(2,1)S(1)} %copy.47), kind=kOutput, calls=%fused_computation.54 | convolution fusion | flops 671088640 | bytes 27787264 | tf_op jit(solution)/shard_map/ikc,jkc->ijc/dot_general | solution.py:152
  589.7 6.0 copy.48
  596.4 50.3 %reduce-scatter.2.cloned.1.call-done = f32[32,64,128]{2,0,1:T(8,128)} async-done(((f32[32,256,128]{2,0,1:T(8,128)}), f32[32,64,128]{2,0,1:T(8,128)}) %reduce-scatter.2.cloned.1.call-update) | async-done | bytes 1048592 | tf_op jit(solution)/shard_map/reduce_scatter | solution.py:158
  646.7 1.7 reduce_sum.94
  648.4 1.9 multiply_reduce_fusion.1
  650.9 1.1 convolution_convert_fusion
  (442 shorter events, 138.1 us)
Async XLA Ops:
  7.2 2.0 copy-start
  7.2 15.2 %copy-start.6 = (f32[4,160,128]{2,1,0:T(8,128)S(1)}, f32[4,160,128]{2,1,0:T(8,128)}, u32[]{:S(2)}) copy-start(f32[4,160,128]{2,1,0:T(8,128)} %param.18) | copy-start | bytes 983044
  7.2 157.4 %all-reduce.2.cloned.1.call-start = ((), (), s32[]{:S(2)}) async-start(), calls=%async_computation.1 | async-start | bytes 3932160 | tf_op jit(solution)/shard_map/psum | solution.py:112
  10.2 11.8 %collective-permute-start = (bf16[48,256]{1,0:T(8,128)(2,1)S(1)}, bf16[48,256]{1,0:T(8,128)(2,1)S(1)}, u32[]{:S(2)}, u32[]{:S(2)}) collective-permute-start(bf16[48,256]{1,0:T(8,128)(2,1)S(1)} %get-tuple-element.126), channel_id=1, source_target_pairs={{0,1},{1,2},{2,3},{3,4},{4,5},{5,6},{6,7},{7,8},{8,9},{9,10},{10,1... | collective-permute-start | bytes 73736 | tf_op jit(solution)/shard_map/ppermute | solution.py:19
  15.1 7.0 %collective-permute-start.1 = (bf16[48,256]{1,0:T(8,128)(2,1)S(1)}, bf16[48,256]{1,0:T(8,128)(2,1)S(1)}, u32[]{:S(2)}, u32[]{:S(2)}) collective-permute-start(bf16[48,256]{1,0:T(8,128)(2,1)S(1)} %get-tuple-element.125), channel_id=1, source_target_pairs={{1,0},{2,1},{3,2},{4,3},{5,4},{6,5},{7,6},{8,7},{9,8},{10,9},{11,1... | collective-permute-start | bytes 73736 | tf_op jit(solution)/shard_map/ppermute | solution.py:20
  22.1 2.5 copy-start.5
  22.2 2.5 copy-start.7
  22.2 2.5 copy-start.8
  28.6 140.7 %copy-start.2 = (bf16[128,1024]{1,0:T(8,128)(2,1)S(1)}, bf16[128,1024]{1,0:T(8,128)(2,1)}, u32[]{:S(2)}) copy-start(bf16[128,1024]{1,0:T(8,128)(2,1)} %param.28) | copy-start | bytes 786436
  28.6 140.7 %copy-start.3 = (bf16[128,512]{1,0:T(8,128)(2,1)S(1)}, bf16[128,512]{1,0:T(8,128)(2,1)}, u32[]{:S(2)}) copy-start(bf16[128,512]{1,0:T(8,128)(2,1)} %param.30) | copy-start | bytes 393220
  28.6 547.3 %all-gather.2.cloned.1.call-start = ((), (), s32[]{:S(2)}) async-start(), calls=%async_computation.2 | async-start | bytes 28311552 | tf_op jit(solution)/shard_map/all_gather | solution.py:155
  166.4 2.9 copy-start.4
  357.1 289.6 %reduce-scatter.2.cloned.1.call-start = ((), (), s32[]{:S(2)}) async-start(), calls=%async_computation.3 | async-start | bytes 5242880 | tf_op jit(solution)/shard_map/reduce_scatter | solution.py:158
  595.7 55.2 %copy-start.9 = (bf16[128,128]{1,0:T(8,128)(2,1)S(1)}, bf16[128,128]{1,0:T(8,128)(2,1)}, u32[]{:S(2)}) copy-start(bf16[128,128]{1,0:T(8,128)(2,1)} %param.31) | copy-start | bytes 98308
  646.7 3.6 copy-start.1
Sparse Core Ops, SparseCore 0:
  28.7 135.7 all-reduce.1
  357.2 218.6 all-gather.1
  595.8 50.8 reduce-scatter.1
where the time goes:
time: 663 us; the launch traced here: 659 us
  waiting for transfers between devices  401 us (60%)
  other arithmetic  106 us (16%)
  matrix products  85.3 us (13%)
  local copies, waits for them, and re-layouts  43.3 us (7%)
  between operations  16.1 us (2%)
    all_gather x1, waiting for transfers between devices, body(): lax.all_gather(right_ops, 'row', axis=0, tiled=True)  215 us
    psum x1, waiting for transfers between devices, body(): totals = lax.psum(table_sums, ('row', 'col'))  136 us
    reduce_scatter x1, waiting for transfers between devices, body(): lax.psum_scatter(partial_value, 'col', scatter_dimension=1, tiled=True)  50.3 us
    dot_general x32, matrix products, pair_row(): jnp.dot(inner, trans_out, preferred_element_type=jnp.float32)  42.2 us
    reduce_sum x34, other arithmetic, normalize(): average = jnp.mean(values, axis=-1, keepdims=True)  35.6 us
    mul x33, local copies, waits for them, and re-layouts, normalize(): return centered * lax.rsqrt(variance + EPS) * gain_row  25.1 us
    dynamic_update_slice x32, other arithmetic, body(): left_ops, right_ops = lax.map(pair_row, (pair_in, row_terms))  24.9 us
    convert_element_type x32, other arithmetic, body(): col_mask = (col_place * tok_col + jnp.arange(tok_col, dtype=jnp.int32) <...  21.4 us
  transfers between devices with their start and end apart: 5, of which 3 were waited for; matrix products, arithmetic and copies ran while one was open for 1% of the time, Pallas kernels for 0%

commit v1 on v0

--- a/solution.py
+++ b/solution.py
@@ -109,7 +109,8 @@
     table_sums = jnp.zeros((tokens + atom_rows, hidden.shape[1]), jnp.float32)
     table_sums = lax.dynamic_update_slice_in_dim(table_sums, window, first_token, 0)[:tokens]
     count_float = atom_counts.astype(jnp.float32)
-    totals = lax.psum(table_sums, ("row", "col"))
+    parts = lax.all_gather(table_sums, ("row", "col"))
+    totals = jnp.sum(parts, axis=0)
     single_all = (totals / count_float[:, None]).astype(jnp.bfloat16)
     row_dev, tok_col, channels = pair_in.shape
     col_place = lax.axis_index("col")

time: 663 us -> 828 us (1.25)
  waiting for transfers between devices: 401 us -> 604 us
  matrix products: 85.3 us -> 53.9 us
  local copies, waits for them, and re-layouts: 43.3 us -> 21 us
  other arithmetic: 106 us -> 124 us
    all_gather x0 -> x1, waiting for transfers between devices: none -> 339 us  [body(): parts = lax.all_gather(table_sums, ('row', 'col'))]
    psum x1 -> x0, waiting for transfers between devices: 136 us -> none  [body(): totals = lax.psum(table_sums, ('row', 'col'))]
    dot_general x32, matrix products: 42.2 us -> 13.3 us  [pair_row(): jnp.dot(inner, trans_out, preferred_element_type=jnp.float32)]
    mul x33, local copies, waits for them, and re-layouts: 25.1 us -> 0.24 us  [normalize(): return centered * lax.rsqrt(variance + EPS) * gain_row]
    reduce_sum x0 -> x1, other arithmetic: none -> 19.8 us  [body(): totals = jnp.sum(parts, axis=0)]
where the time goes in v1:
time: 828 us; the launch traced here: 826 us
  waiting for transfers between devices  604 us (73%)
  other arithmetic  124 us (15%)
  matrix products  53.9 us (7%)
  local copies, waits for them, and re-layouts  21 us (3%)
  between operations  16.2 us (2%)
    all_gather x1, waiting for transfers between devices, body(): parts = lax.all_gather(table_sums, ('row', 'col'))  339 us
    all_gather x1, waiting for transfers between devices, body(): lax.all_gather(right_ops, 'row', axis=0, tiled=True)  214 us
    reduce_scatter x1, waiting for transfers between devices, body(): lax.psum_scatter(partial_value, 'col', scatter_dimension=1, tiled=True)  51 us
    reduce_sum x34, other arithmetic, normalize(): average = jnp.mean(values, axis=-1, keepdims=True)  35.6 us
    dynamic_update_slice x32, other arithmetic, body(): left_ops, right_ops = lax.map(pair_row, (pair_in, row_terms))  25.1 us
    convert_element_type x32, other arithmetic, body(): col_mask = (col_place * tok_col + jnp.arange(tok_col, dtype=jnp.int32) <...  21.4 us
    reduce_sum x1, other arithmetic, body(): totals = jnp.sum(parts, axis=0)  19.8 us
    reduce_sum x66, other arithmetic, normalize(): variance = jnp.mean(centered * centered, axis=-1, keepdims=True)  17.2 us
  transfers between devices with their start and end apart: 5, of which 3 were waited for; matrix products, arithmetic and copies ran while one was open for 1% of the time, Pallas kernels for 0%

profile of v1, /device:TPU:0, one launch (start us, length us, event | category | flops | bytes accessed | tf_op | source)
XLA Modules:
  0.0 826.2 jit_solution(17797780901890282111)
XLA Ops:
  7.2 0.9 convert_reduce_fusion.2
  8.2 1.0 fusion.52
  9.2 1.0 fusion.95
  10.2 4.8 collective-permute-start
  15.1 1.3 collective-permute-start.1
  16.4 1.0 reduce-window.9
  17.6 0.8 fusion.94
  23.1 1.2 convolution_bitcast_fusion.1
  25.4 1.8 dynamic_update_slice.10
  27.2 1.4 slice.138
  28.7 338.7 %all-gather.6.cloned.1.call-done = f32[40960,384]{1,0:T(8,128)} async-done(((f32[1280,384]{1,0:T(8,128)}), f32[40960,384]{1,0:T(8,128)}) %all-gather.6.cloned.1.call-update) | async-done | bytes 62914576 | tf_op jit(solution)/shard_map/all_gather | solution.py:112
  367.4 19.8 %reduce_sum.103 = f32[1280,384]{1,0:T(8,128)S(1)} reduce(f32[32,1280,384]{2,1,0:T(8,128)} %bitcast.78, f32[]{:T(128)} %constant.35.clone.1), dimensions={0}, to_apply=%region_7.8 | reduce | flops 15237120 | bytes 64880644 | tf_op jit(solution)/shard_map/reduce_sum | solution.py:113
  388.9 131.5 %while.13 = (s32[]{:T(128)}, bf16[32,320,128]{2,1,0:T(8,128)(2,1)}, bf16[32,320,128]{2,1,0:T(8,128)(2,1)}, bf16[32,320,128]{2,1,0:T(8,128)(2,1)}, f32[32,128]{1,...) while((s32[]{:T(128)}, bf16[32,320,128]{2,1,0:T(8,128)(2,1)}, ...), condition=%wide.region_13.14_spmd.clone, body=%wide.region_8.13_spmd.clone.sunk | while | flops 170354240 | bytes 5716109 | solution.py:152
  388.9 1.0 convert_reduce_fusion.4
  392.2 0.8 bitcast_dynamic-update-slice_fusion.3
  393.0 1.0 convert_reduce_fusion.4
  397.1 1.0 convert_reduce_fusion.4
  401.2 1.0 convert_reduce_fusion.4
  405.3 1.0 convert_reduce_fusion.4
  409.4 1.0 convert_reduce_fusion.4
  413.5 1.0 convert_reduce_fusion.4
  416.8 0.8 bitcast_dynamic-update-slice_fusion.3
  417.6 1.0 convert_reduce_fusion.4
  421.7 1.0 convert_reduce_fusion.4
  425.8 1.0 convert_reduce_fusion.4
  429.9 1.0 convert_reduce_fusion.4
  433.3 0.8 bitcast_dynamic-update-slice_fusion.3
  434.1 1.0 convert_reduce_fusion.4
  438.2 1.0 convert_reduce_fusion.4
  441.5 0.8 bitcast_dynamic-update-slice_fusion.3
  442.3 1.0 convert_reduce_fusion.4
  445.6 0.8 bitcast_dynamic-update-slice_fusion.3
  446.4 1.0 convert_reduce_fusion.4
  450.5 1.0 convert_reduce_fusion.4
  454.7 1.0 convert_reduce_fusion.4
  458.8 1.0 convert_reduce_fusion.4
  462.1 0.8 bitcast_dynamic-update-slice_fusion.3
  462.9 1.0 convert_reduce_fusion.4
  467.0 1.0 convert_reduce_fusion.4
  470.3 0.8 bitcast_dynamic-update-slice_fusion.3
  471.1 1.0 convert_reduce_fusion.4
  475.2 1.0 convert_reduce_fusion.4
  479.3 1.0 convert_reduce_fusion.4
  482.6 0.8 bitcast_dynamic-update-slice_fusion.3
  483.4 1.0 convert_reduce_fusion.4
  486.7 0.8 bitcast_dynamic-update-slice_fusion.3
  487.5 1.0 convert_reduce_fusion.4
  490.9 0.8 bitcast_dynamic-update-slice_fusion.3
  491.7 1.0 convert_reduce_fusion.4
  495.8 1.0 convert_reduce_fusion.4
  499.8 1.0 convert_reduce_fusion.4
  503.9 1.0 convert_reduce_fusion.4
  508.0 1.0 convert_reduce_fusion.4
  512.1 1.0 convert_reduce_fusion.4
  516.3 1.0 convert_reduce_fusion.4
  520.4 5.0 copy.46
  525.4 3.8 copy.47
  529.2 214.3 %all-gather.4.cloned.1.call-done = bf16[256,320,128]{1,0,2:T(8,128)(2,1)} async-done(((bf16[32,320,128]{1,0,2:T(8,128)(2,1)}), bf16[256,320,128]{1,0,2:T(8,128)(2,1)}) %all-gather.4.cloned.1.call-update) | async-done | bytes 20971536 | tf_op jit(solution)/shard_map/all_gather | solution.py:156
  743.6 13.8 %convolution_bitcast_fusion = f32[32,256,128]{1,0,2:T(8,128)} fusion(bf16[256,320,128]{1,0,2:T(8,128)(2,1)} %all-gather.4.cloned.1.call-done, bf16[32,320,128]{1,0,2:T(8,128)(2,1)S(1)} %copy.47), kind=kOutput, calls=%fused_computation.54 | convolution fusion | flops 671088640 | bytes 27787264 | tf_op jit(solution)/shard_map/ikc,jkc->ijc/dot_general | solution.py:153
  757.3 6.0 copy.48
  763.4 51.0 %reduce-scatter.2.cloned.1.call-done = f32[32,64,128]{2,0,1:T(8,128)} async-done(((f32[32,256,128]{2,0,1:T(8,128)}), f32[32,64,128]{2,0,1:T(8,128)}) %reduce-scatter.2.cloned.1.call-update) | async-done | bytes 1048592 | tf_op jit(solution)/shard_map/reduce_scatter | solution.py:159
  814.4 1.7 reduce_sum.104
  816.0 1.9 multiply_reduce_fusion.1
  818.6 1.1 convolution_convert_fusion
  (451 shorter events, 95.9 us)
Async XLA Ops:
  7.2 2.0 copy-start
  7.2 15.3 %copy-start.7 = (f32[4,160,128]{2,1,0:T(8,128)S(1)}, f32[4,160,128]{2,1,0:T(8,128)}, u32[]{:S(2)}) copy-start(f32[4,160,128]{2,1,0:T(8,128)} %param.18) | copy-start | bytes 983044
  7.2 360.2 %all-gather.6.cloned.1.call-start = ((), (), s32[]{:S(2)}) async-start(), calls=%async_computation.3 | async-start | bytes 64880640 | tf_op jit(solution)/shard_map/all_gather | solution.py:112
  10.2 11.8 %collective-permute-start = (bf16[48,256]{1,0:T(8,128)(2,1)S(1)}, bf16[48,256]{1,0:T(8,128)(2,1)S(1)}, u32[]{:S(2)}, u32[]{:S(2)}) collective-permute-start(bf16[48,256]{1,0:T(8,128)(2,1)S(1)} %get-tuple-element.126), channel_id=1, source_target_pairs={{0,1},{1,2},{2,3},{3,4},{4,5},{5,6},{6,7},{7,8},{8,9},{9,10},{10,1... | collective-permute-start | bytes 73736 | tf_op jit(solution)/shard_map/ppermute | solution.py:19
  15.1 7.0 collective-permute-start.1
  22.1 2.5 copy-start.6
  22.2 2.5 copy-start.9
  22.2 2.5 copy-start.10
  28.7 714.9 %all-gather.4.cloned.1.call-start = ((), (), s32[]{:S(2)}) async-start(), calls=%async_computation.1 | async-start | bytes 28311552 | tf_op jit(solution)/shard_map/all_gather | solution.py:156
  387.3 0.9 copy-start.8
  387.3 1.3 copy-start.3
  387.3 1.3 copy-start.4
  387.3 1.3 copy-start.12
  387.3 1.3 copy-start.13
  388.2 0.7 copy-start.5
  525.4 289.0 %reduce-scatter.2.cloned.1.call-start = ((), (), s32[]{:S(2)}) async-start(), calls=%async_computation.2 | async-start | bytes 5242880 | tf_op jit(solution)/shard_map/reduce_scatter | solution.py:159
  763.3 55.2 %copy-start.11 = (bf16[128,128]{1,0:T(8,128)(2,1)S(1)}, bf16[128,128]{1,0:T(8,128)(2,1)}, u32[]{:S(2)}) copy-start(bf16[128,128]{1,0:T(8,128)(2,1)} %param.31) | copy-start | bytes 98308
  763.3 56.3 %copy-start.1 = (bf16[128,512]{1,0:T(8,128)(2,1)S(1)}, bf16[128,512]{1,0:T(8,128)(2,1)}, u32[]{:S(2)}) copy-start(bf16[128,512]{1,0:T(8,128)(2,1)} %param.23) | copy-start | bytes 393220
  814.4 3.6 copy-start.2
Sparse Core Ops, SparseCore 0:
  28.8 338.5 all-gather.5
  525.5 218.0 all-gather.3
  763.4 50.8 reduce-scatter.1
